TPU v7x, 32 devices: a whole 2x2x4 slice. The times are simulated.
32 devices in a mesh: ctx: 2 (over y), exp: 16 (over z, x, core).
Axes of the slice: x: 2, y: 2, z: 4, core: 2. Of those that a mesh axis runs over, the one named last changes fastest.
Arguments:
- residual: bfloat16 [16, 128, 2048], P('exp', 'ctx'), may hold values from -1 to 1
- queries: bfloat16 [16, 128, 2048], P('exp', 'ctx'), may hold values from -6 to 6
- key_rows: bfloat16 [16, 128, 256], P('exp', 'ctx'), may hold values from -6 to 6
- value_rows: bfloat16 [16, 128, 256], P('exp', 'ctx'), may hold values from -0.8984375 to 0.8984375
- span_order: int32 [4], replicated, may hold values from 0 to 3, as said below
- norm_gain: float32 [2048], replicated, may hold values from 0.1 to 1.9
- gate_logits: float32 [16, 128, 8], P('exp', 'ctx'), may hold values from -6 to 6
- expert_ids: int32 [16, 128, 8], P('exp', 'ctx'), may hold values from 0 to 15, all different within a row; in each aligned block of 64 rows (0 to 63, 64 to 127, ..., all dimensions but the last counted through in order) at most 32 rows name the same one
- gate_up: bfloat16 [16, 2048, 768], P('exp'), may hold values from -1 to 1
- down_weight: bfloat16 [16, 384, 2048], P('exp'), may hold values from -0.3125 to 0.3125
Outputs:
- layer_out: bfloat16 [16, 128, 2048], P('exp', 'ctx')
Inputs may be any that keep to these rules, and one draw needn't show every extreme that they name: A permutation of 0 to 3; rows b * 32 to b * 32 + 31 of every sequence hold positions span_order[b] * 32 onward. `expert_ids`: each token names 8 different experts; within the 64 rows of one device (aligned blocks of rows) no expert is named by more than 32 tokens.
All inputs are finite; a program needn't handle non-finite values.
Results may differ from a plain program's by a relative error of at most 0.0062.
Values may be sent and summed in bfloat16 or wider, within the bound.
A program may use at most 64 MiB of HBM per device.

v0:
```python
import math

import jax
import jax.numpy as jnp
from jax import lax
from jax.sharding import PartitionSpec as P

KVH = 2
HD = 128
GROUP = 8
HALF = 32


big_negative = -1e30
norm_eps = 1e-06


def span_positions(span_order, first_row, row_total):
    row_index = first_row + jnp.arange(row_total, dtype=jnp.int32)
    onehot = (row_index // HALF)[:, None] == jnp.arange(span_order.shape[0], dtype=jnp.int32)[
        None, :
    ]
    block_start = jnp.sum(jnp.where(onehot, span_order[None, :], 0), axis=1)
    return block_start * HALF + row_index % HALF


def attend_update(state_in, pieces, first_index, query_heads, query_pos, span_order):
    running_max, running_sum, running_out = state_in
    key_piece, value_piece = pieces
    key_count = key_piece.shape[1]
    key_heads = key_piece[0].reshape(key_count, KVH, HD)
    value_heads = value_piece[0].reshape(key_count, KVH, HD)
    key_pos = span_positions(span_order, first_index, key_count)
    score_scale = 1.0 / math.sqrt(HD)
    scores = (
        jnp.einsum("tgqd,cgd->gqtc", query_heads, key_heads, preferred_element_type=jnp.float32)
        * score_scale
    )
    visible = (key_pos[None, :] <= query_pos[:, None])[None, None]
    scores = jnp.where(visible, scores, big_negative)
    new_max = jnp.maximum(running_max, jnp.max(scores, axis=3))
    weights = jnp.where(visible, jnp.exp(scores - new_max[..., None]), 0.0)
    new_sum = jnp.sum(weights, axis=3)
    product = jnp.einsum(
        "gqtc,cgd->tgqd",
        weights.astype(jnp.bfloat16),
        value_heads,
        preferred_element_type=jnp.float32,
    )
    return (new_max, new_sum, product)


def run_expert(arrived, gate_up, down_weight):
    sources, slots, width = arrived.shape
    rows_in = arrived.reshape(sources * slots, width)
    projected = jnp.dot(rows_in, gate_up[0], preferred_element_type=jnp.float32)
    hidden_units = gate_up.shape[2] // 2
    hidden = (jax.nn.silu(projected[:, :hidden_units]) * projected[:, hidden_units:]).astype(
        jnp.bfloat16
    )
    result = jnp.dot(hidden, down_weight[0], preferred_element_type=jnp.float32).astype(
        jnp.bfloat16
    )
    return result.reshape(sources, slots, width)


def local(
    residual,
    queries,
    key_rows,
    value_rows,
    span_order,
    norm_gain,
    gate_logits,
    expert_ids,
    gate_up,
    down_weight,
):
    tokens_here = residual.shape[1]
    model_width = residual.shape[2]
    ctx_index = lax.axis_index("ctx")
    query_pos = span_positions(span_order, ctx_index * tokens_here, tokens_here)
    query_heads = queries[0].reshape(tokens_here, KVH, GROUP, HD)
    state_shape = (KVH, GROUP, tokens_here)
    initial = (
        jnp.full(state_shape, big_negative, jnp.float32),
        jnp.zeros(state_shape, jnp.float32),
        jnp.zeros((tokens_here, KVH, GROUP, HD), jnp.float32),
    )
    final_state = attend_update(
        initial,
        (
            lax.all_gather(key_rows, "ctx", axis=1, tiled=True),
            lax.all_gather(value_rows, "ctx", axis=1, tiled=True),
        ),
        jnp.int32(0),
        query_heads,
        query_pos,
        span_order,
    )
    running_sum = final_state[1]
    attention = (final_state[2] / jnp.transpose(running_sum, (2, 0, 1))[..., None]).reshape(
        tokens_here, -1
    )
    attention = lax.optimization_barrier(attention.astype(jnp.bfloat16)).astype(jnp.float32)
    mixed_rows = residual[0].astype(jnp.float32) + attention
    scale_rms = lax.rsqrt(jnp.mean(mixed_rows * mixed_rows, axis=1, keepdims=True) + norm_eps)
    normed = (mixed_rows * scale_rms * norm_gain).astype(jnp.bfloat16)
    raised = jnp.exp(gate_logits[0])
    routing_weight = raised / jnp.sum(raised, axis=1, keepdims=True)
    destinations = lax.axis_size("exp")
    top_count = expert_ids.shape[2]
    mean_load = tokens_here * top_count // destinations
    with_slack = mean_load + tokens_here * top_count // (4 * destinations)
    capacity = min(
        tokens_here, max(2, max(mean_load, min(with_slack, 524288 // (destinations * model_width))))
    )
    flat_experts = expert_ids[0].reshape(-1)
    owner_onehot = (
        flat_experts[:, None] == jnp.arange(destinations, dtype=jnp.int32)[None, :]
    ).astype(jnp.int32)
    earlier = jnp.cumsum(owner_onehot, axis=0) - owner_onehot
    slot_rank = jnp.sum(earlier * owner_onehot, axis=1)
    target_slot = flat_experts * capacity + slot_rank
    placement = (
        target_slot[:, None] == jnp.arange(destinations * capacity, dtype=jnp.int32)[None, :]
    ).astype(jnp.int32)
    token_map = placement.reshape(tokens_here, top_count, -1).sum(axis=1).astype(jnp.bfloat16)
    outgoing = jnp.einsum(
        "ts,td->sd", token_map, normed, preferred_element_type=jnp.float32
    ).astype(jnp.bfloat16)
    outgoing = outgoing.reshape(destinations, capacity, -1)
    arrived = lax.all_to_all(outgoing, "exp", split_axis=0, concat_axis=0, tiled=True)
    returned = lax.all_to_all(
        run_expert(arrived, gate_up, down_weight), "exp", split_axis=0, concat_axis=0, tiled=True
    )
    returned_rows = returned.reshape(destinations * capacity, -1)
    picked = (
        jnp.take(returned_rows, target_slot, axis=0)
        .astype(jnp.float32)
        .reshape(tokens_here, top_count, -1)
    )
    combined = jnp.sum(picked * routing_weight[:, :, None], axis=1)
    layer_out = (mixed_rows + combined).astype(jnp.bfloat16)
    return layer_out[None]


def solution(mesh):
    return jax.shard_map(
        local,
        mesh=mesh,
        in_specs=(
            P("exp", "ctx", None),
            P("exp", "ctx", None),
            P("exp", "ctx", None),
            P("exp", "ctx", None),
            P(),
            P(),
            P("exp", "ctx", None),
            P("exp", "ctx", None),
            P("exp", None, None),
            P("exp", None, None),
        ),
        out_specs=P("exp", "ctx", None),
        check_vma=False,
    )
```

profile of v0, /device:TPU:11, one launch (start us, length us, event | category | flops | bytes accessed | tf_op | source)
XLA Modules:
  0.0 144.3 jit_solution(2318185665745731534)
XLA Ops:
  0.0 0.9 copy.54
  0.9 0.1 eq.76
  1.0 0.1 reshape_squeeze.15
  1.1 0.7 select_reduce_fusion
  1.9 0.7 select_reduce_fusion.1
  2.6 1.0 copy.69
  3.6 3.6 %all_gather.6 = bf16[1,128,256]{2,1,0:T(8,128)(2,1)S(1)} all-gather(bf16[1,64,256]{2,1,0:T(8,128)(2,1)} %param.12), channel_id=1, replica_groups=mesh['ctx'=2,'exp'=16] {'ctx'}, dimensions={1}, use_global_device_ids=true | all-gather | bytes 98304 | tf_op jit(solution)/shard_map/all_gather | solution.py:93
  7.3 0.1 copy.48
  7.5 1.0 fusion.30
  8.5 3.6 %all_gather.7 = bf16[1,128,256]{2,1,0:T(8,128)(2,1)S(1)} all-gather(bf16[1,64,256]{2,1,0:T(8,128)(2,1)} %param.13), channel_id=1, replica_groups=mesh['ctx'=2,'exp'=16] {'ctx'}, dimensions={1}, use_global_device_ids=true | all-gather | bytes 98304 | tf_op jit(solution)/shard_map/all_gather | solution.py:94
  12.1 0.1 copy.51
  12.2 1.5 %fusion.8 = f32[2,8,64]{2,1,0:T(8,128)S(1)} fusion(f32[2,8,64,128]{3,2,1,0:T(8,128)} %get-tuple-element.8, f32[2,8,64]{2,1,0:T(8,128)S(1)} %broadcast_maximum_fusion, pred[64,128]{1,0:T(8,128)(4,1)S(1)} %broadcast_compare_fusion), kind=kLoop, calls=%fused_computation.23 | loop fusion | flops 392192 | bytes 540672 | tf_op jit(solution)/shard_map/reduce_sum | solution.py:43
  13.8 1.4 fusion.6
  15.2 0.2 copy.53
  15.4 0.2 multiply_reduce_fusion.1
  15.7 1.2 reduce-window.6
  16.8 0.2 slice_reduce_fusion
  17.1 0.1 fusion.24
  17.2 0.1 reduce_sum.80
  17.4 0.4 convert_reduce_fusion
  17.8 1.7 %convolution_convert_fusion.1 = bf16[512,2048]{1,0:T(8,128)(2,1)S(1)} fusion(bf16[64,2048]{1,0:T(8,128)(2,1)S(1)} %bitcast.85, bf16[1,64,2048]{2,1,0:T(8,128)(2,1)} %param.10, f32[2048]{0:T(1024)S(1)} %copy-done.5, f32[64]{0:T(128)S(1)} %add_rsqrt_fusion, s32[64,512]{1,0:T(8,128)S(1)} %convert_reduce_fusion), kind=kOutput, calls=%fused_computation.5 | convolution fusion | flops 136085504 | bytes 2760960 | tf_op jit(solution)/shard_map/ts,td->sd/dot_general | solution.py:129
  19.5 55.9 %all_to_all.10 = bf16[16,32,2048]{2,1,0:T(8,128)(2,1)S(1)} all-to-all(bf16[16,32,2048]{2,1,0:T(8,128)(2,1)S(1)} %bitcast.83), channel_id=1, replica_groups=mesh['ctx'=2,'exp'=16] {'exp'}, dimensions={0} | all-to-all | bytes 4194304 | tf_op jit(solution)/shard_map/all_to_all | solution.py:133
  75.4 1.8 %fusion = f32[512,768]{1,0:T(8,128)S(1)} fusion(bf16[512,2048]{1,0:T(8,128)(2,1)S(1)} %bitcast.88, bf16[1,2048,768]{2,1,0:T(8,128)(2,1)S(1)} %copy-done), kind=kOutput, calls=%fused_computation.2 | convolution fusion | flops 1610612736 | bytes 6815744 | tf_op jit(solution)/shard_map/dot_general | solution.py:56
  77.2 2.6 %convolution_convert_fusion = bf16[512,2048]{1,0:T(8,128)(2,1)} fusion(bf16[1,384,2048]{2,1,0:T(8,128)(2,1)S(1)} %copy-done.6, f32[512,768]{1,0:T(8,128)S(1)} %fusion), kind=kOutput, calls=%fused_computation.4 | convolution fusion | flops 807534592 | bytes 5242880 | tf_op jit(solution)/shard_map/dot_general | solution.py:61
  79.8 5.2 %all-to-all-start.1 = ((bf16[16,32,2048]{2,1,0:T(8,128)(2,1)}), bf16[16,32,2048]{2,1,0:T(8,128)(2,1)}, u32[]{:S(2)}, u32[]{:S(2)}) async-start(bf16[16,32,2048]{2,1,0:T(8,128)(2,1)} %bitcast.87), calls=%async_computation.1 | async-start | bytes 4194304 | tf_op jit(solution)/shard_map/all_to_all | solution.py:134
  85.1 0.1 mul.107
  85.2 0.1 copy.58
  85.3 0.1 copy.61
  85.4 47.1 %all-to-all-done.1 = bf16[16,32,2048]{2,1,0:T(8,128)(2,1)} async-done(((bf16[16,32,2048]{2,1,0:T(8,128)(2,1)}), bf16[16,32,2048]{2,1,0:T(8,128)(2,1)}, u32[]{:S(2)}, u32[]{:S(2)}) %all-to-all-start.1) | async-done | bytes 2097184 | tf_op jit(solution)/shard_map/all_to_all | solution.py:134
  132.5 7.1 %gather_fusion = bf16[512,2048]{1,0:T(8,128)(2,1)} fusion(bf16[512,2048]{1,0:T(8,128)(2,1)} %bitcast.15, s32[1024]{0:T(1024)S(1)} %pad_clamp_fusion), kind=kCustom, calls=%fused_computation | custom fusion | bytes 4196352 | tf_op jit(solution)/shard_map/jit(_take)/gather | solution.py:139
  139.6 3.9 %multiply_reduce_fusion = f32[64,2048]{1,0:T(8,128)S(1)} fusion(bf16[512,2048]{1,0:T(8,128)(2,1)} %gather_fusion, f32[64,8]{1,0:T(8,128)S(1)} %copy.61, pred[64,8]{1,0:T(8,128)(4,1)S(1)} %copy.58), kind=kLoop, calls=%fused_computation.1 | loop fusion | flops 4063232 | bytes 2624000 | tf_op jit(solution)/shard_map/reduce_sum | solution.py:143
  143.5 0.8 fusion.13
  (34 shorter events, 0.6 us)
Async XLA Ops:
  0.0 75.4 %copy-start = (bf16[1,2048,768]{2,1,0:T(8,128)(2,1)S(1)}, bf16[1,2048,768]{2,1,0:T(8,128)(2,1)}, u32[]{:S(2)}) copy-start(bf16[1,2048,768]{2,1,0:T(8,128)(2,1)} %param.18) | copy-start | bytes 9437188
  12.2 3.2 %copy-start.1 = (bf16[1,64,2048]{2,1,0:T(8,128)(2,1)S(1)}, bf16[1,64,2048]{2,1,0:T(8,128)(2,1)}, u32[]{:S(2)}) copy-start(bf16[1,64,2048]{2,1,0:T(8,128)(2,1)} %param.10) | copy-start | bytes 786436
  13.7 3.6 %copy-start.3 = (s32[1,64,8]{1,2,0:T(8,128)S(1)}, s32[1,64,8]{1,2,0:T(8,128)}, u32[]{:S(2)}) copy-start(s32[1,64,8]{1,2,0:T(8,128)} %param.17) | copy-start | bytes 6148
  13.8 4.1 %copy-start.5 = (f32[2048]{0:T(1024)S(1)}, f32[2048]{0:T(1024)}, u32[]{:S(2)}) copy-start(f32[2048]{0:T(1024)} %param.15) | copy-start | bytes 24580
  75.4 1.8 %copy-start.6 = (bf16[1,384,2048]{2,1,0:T(8,128)(2,1)S(1)}, bf16[1,384,2048]{2,1,0:T(8,128)(2,1)}, u32[]{:S(2)}) copy-start(bf16[1,384,2048]{2,1,0:T(8,128)(2,1)} %param.19) | copy-start | bytes 4718596
  79.8 5.5 %copy-start.4 = (f32[1,64,8]{1,2,0:T(8,128)S(1)}, f32[1,64,8]{1,2,0:T(8,128)}, u32[]{:S(2)}) copy-start(f32[1,64,8]{1,2,0:T(8,128)} %param.16) | copy-start | bytes 6148
  79.8 52.7 %all-to-all-start.1 = ((bf16[16,32,2048]{2,1,0:T(8,128)(2,1)}), bf16[16,32,2048]{2,1,0:T(8,128)(2,1)}, u32[]{:S(2)}, u32[]{:S(2)}) async-start(bf16[16,32,2048]{2,1,0:T(8,128)(2,1)} %bitcast.87), calls=%async_computation.1 | async-start | bytes 4194304 | tf_op jit(solution)/shard_map/all_to_all | solution.py:134
  139.6 3.9 %copy-start.2 = (bf16[1,64,2048]{2,1,0:T(8,128)(2,1)S(1)}, bf16[1,64,2048]{2,1,0:T(8,128)(2,1)}, u32[]{:S(2)}) copy-start(bf16[1,64,2048]{2,1,0:T(8,128)(2,1)} %param.10) | copy-start | bytes 786436
where the time goes:
time: 145 us; the launch traced here: 144 us
  blocking collectives  63.2 us (44%)
  waiting for transfers between devices  47.1 us (32%)
  local copies, waits for them, and re-layouts  10.5 us (7%)
  other arithmetic  9.65 us (7%)
  matrix products  8.49 us (6%)
  starting transfers between devices  5.17 us (4%)
    all_to_all x1, blocking collectives, local(): lax.all_to_all(outgoing, 'exp', split_axis=0, concat_axis=0, tiled=True)  55.9 us
    all_to_all x1, waiting for transfers between devices, local(): lax.all_to_all(run_expert(arrived, gate_up, down_weight), 'exp', split_ax...  47.1 us
    gather x1, local copies, waits for them, and re-layouts, local(): jnp.take(returned_rows, target_slot, axis=0).astype(jnp.float32)  7.1 us
    all_to_all x1, starting transfers between devices, local(): lax.all_to_all(run_expert(arrived, gate_up, down_weight), 'exp', split_ax...  5.17 us
    reduce_sum x1, other arithmetic, local(): combined = jnp.sum(picked * routing_weight[:, :, None], axis=1)  3.86 us
    all_gather x1, blocking collectives, local(): lax.all_gather(key_rows, 'ctx', axis=1, tiled=True)  3.64 us
    all_gather x1, blocking collectives, local(): lax.all_gather(value_rows, 'ctx', axis=1, tiled=True)  3.63 us
  transfers between devices with their start and end apart: 1, of which 1 were waited for; matrix products, arithmetic and copies ran while one was open for 0% of the time, Pallas kernels for 0%

commit v1 on v0

v1 whole, which is shorter than its diff:
```python
import functools
import math

import jax
import jax.numpy as jnp
from jax import lax
from jax.experimental import pallas as pl
from jax.experimental.pallas import tpu as pltpu
from jax.sharding import PartitionSpec as P

MESH = pl.DeviceIdType.MESH
HD = 128
big_negative = -1e30
norm_eps = 1e-06
f32 = jnp.float32
bf16 = jnp.bfloat16


def block_positions(span_ref, row_index, rows_per_span):
    which = row_index // rows_per_span
    start = jnp.zeros_like(row_index)
    for b in range(span_ref.shape[0]):
        start = jnp.where(which == b, span_ref[b], start)
    return start * rows_per_span + row_index % rows_per_span


def kernel(
    n, n_ctx,
    residual, queries, key_rows, value_rows, span_order, norm_gain, gate_logits, expert_ids,
    gate_up, down_weight,
    out,
    keys, values, mixed, xg, wg, yb, r1, r2, r3, gu, dw,
    wsem, kv_send, kv_recv, gs, gr, ws, wr, s1, q1, s2, q2, s3, q3u, q3d,
):
    A = n // 4
    tokens = residual.shape[1]
    width = residual.shape[2]
    kvh = key_rows.shape[2] // HD
    group = width // HD // kvh
    me = lax.axis_index("exp")
    ctx = lax.axis_index("ctx")
    c = me % 2
    x = (me // 2) % 2
    z = me // 4

    def idx(zz, xx, cc):
        return (zz * 2 + xx) * 2 + cc

    core_peer = idx(z, x, 1 - c)
    x_peer = idx(z, 1 - x, c)
    up_peer = jnp.minimum(z + 1, A - 1) * 4 + x * 2 + c
    dn_peer = jnp.maximum(z - 1, 0) * 4 + x * 2 + c
    has_up = z < A - 1
    has_dn = z > 0

    gu_copy = pltpu.make_async_copy(gate_up.at[0], gu, wsem.at[0])
    dw_copy = pltpu.make_async_copy(down_weight.at[0], dw, wsem.at[1])
    gu_copy.start()
    dw_copy.start()

    barrier = pltpu.get_barrier_semaphore()
    for k in range(1, n_ctx):
        pl.semaphore_signal(
            barrier, inc=1, device_id={"ctx": (ctx + k) % n_ctx}, device_id_type=MESH
        )
    for peer in (core_peer, x_peer):
        pl.semaphore_signal(barrier, inc=1, device_id={"exp": peer}, device_id_type=MESH)

    @pl.when(has_up)
    def _():
        pl.semaphore_signal(barrier, inc=1, device_id={"exp": up_peer}, device_id_type=MESH)

    @pl.when(has_dn)
    def _():
        pl.semaphore_signal(barrier, inc=1, device_id={"exp": dn_peer}, device_id_type=MESH)

    pl.semaphore_wait(barrier, n_ctx + 1 + jnp.where(has_up, 1, 0) + jnp.where(has_dn, 1, 0))

    def kv_copies(k):
        target = {"ctx": (ctx + k) % n_ctx}
        return [
            pltpu.make_async_remote_copy(
                src.at[0], dst.at[ctx], kv_send.at[i, k], kv_recv.at[i, k],
                device_id=target, device_id_type=MESH,
            )
            for i, (src, dst) in enumerate(((key_rows, keys), (value_rows, values)))
        ]

    for k in range(1, n_ctx):
        for cp in kv_copies(k):
            cp.start()
    keys[ctx] = key_rows[0]
    values[ctx] = value_rows[0]

    raised = jnp.exp(gate_logits[0])
    routing = raised / jnp.sum(raised, axis=1, keepdims=True)
    lanes = lax.broadcasted_iota(jnp.int32, (tokens, 128), 1)
    dense = jnp.zeros((tokens, 128), f32)
    for j in range(routing.shape[1]):
        dense = jnp.where(expert_ids[0][:, j : j + 1] == lanes, routing[:, j : j + 1], dense)
    square = jnp.concatenate([dense, jnp.zeros((128 - tokens, 128), f32)], axis=0)
    wg[me] = jnp.transpose(square)[:n]

    total_keys = n_ctx * tokens
    rows_per_span = total_keys // span_order.shape[0]
    query_pos = block_positions(
        span_order, ctx * tokens + lax.broadcasted_iota(jnp.int32, (tokens, 1), 0), rows_per_span
    )
    key_pos = block_positions(
        span_order, lax.broadcasted_iota(jnp.int32, (1, total_keys), 1), rows_per_span
    )
    visible = jnp.where(key_pos <= query_pos, 1, 0)
    visible = jnp.concatenate([visible] * group, axis=0) > 0

    for k in range(1, n_ctx):
        for cp in kv_copies(k):
            cp.wait()

    for g in range(kvh):
        heads = [g * group + i for i in range(group)]
        q = jnp.concatenate([queries[0, :, h * HD : (h + 1) * HD] for h in heads], axis=0)
        kk = keys[:, :, g * HD : (g + 1) * HD].reshape(total_keys, HD)
        vv = values[:, :, g * HD : (g + 1) * HD].reshape(total_keys, HD)
        scores = lax.dot_general(
            q, kk, (((1,), (1,)), ((), ())), preferred_element_type=f32
        ) * (1.0 / math.sqrt(HD))
        scores = jnp.where(visible, scores, big_negative)
        weights = jnp.where(
            visible, jnp.exp(scores - jnp.max(scores, axis=1, keepdims=True)), 0.0
        )
        total = jnp.sum(weights, axis=1, keepdims=True)
        summed = jnp.dot(weights.astype(bf16), vv, preferred_element_type=f32) / total
        summed = summed.astype(bf16).astype(f32)
        for i, h in enumerate(heads):
            cols = slice(h * HD, (h + 1) * HD)
            mixed[:, cols] = (
                residual[0, :, cols].astype(f32) + summed[i * tokens : (i + 1) * tokens]
            )

    rows = mixed[...]
    scale = lax.rsqrt(jnp.mean(rows * rows, axis=1, keepdims=True) + norm_eps)
    xg[me] = (rows * scale * norm_gain[...]).astype(bf16)

    def relay(slot, target, k):
        return [
            pltpu.make_async_remote_copy(
                buf.at[slot], buf.at[slot], send.at[k], recv.at[slot],
                device_id={"exp": target}, device_id_type=MESH,
            )
            for buf, send, recv in ((xg, gs, gr), (wg, ws, wr))
        ]

    def start(copies):
        for cp in copies:
            cp.start()

    def arrive(slot):
        for cp in relay(slot, core_peer, 0):
            cp.wait_recv()

    up_copy = lambda zz: relay(idx(zz, x, c), up_peer, zz)
    dn_copy = lambda zz: relay(idx(zz, x, c), dn_peer, A + zz)
    x_copy = lambda zz: relay(idx(zz, x, c), x_peer, 2 * A + zz)
    core_copy = lambda zz, xx: relay(idx(zz, xx, c), core_peer, 3 * A + zz * 2 + xx)

    def both(t, body):
        def one(s, carry):
            zz = z + t * (1 - 2 * s)
            ok = (zz >= 0) & (zz < A) & ((t > 0) | (s == 0))

            @pl.when(ok)
            def _():
                body(zz, s)

            return carry

        lax.fori_loop(0, 2, one, 0)

    def own_column(zz, s):
        @pl.when(zz != z)
        def _():
            arrive(idx(zz, x, c))

        @pl.when((zz <= z) & has_up)
        def _():
            start(up_copy(zz))

        @pl.when((zz >= z) & has_dn)
        def _():
            start(dn_copy(zz))

        start(x_copy(zz))
        start(core_copy(zz, x))

    def other_column(zz, s):
        arrive(idx(zz, 1 - x, c))
        start(core_copy(zz, 1 - x))

    def r1_copy(zz, xx):
        return pltpu.make_async_remote_copy(
            yb.at[idx(zz, xx, 1 - c)], r1.at[zz * 2 + xx],
            s1.at[zz * 2 + xx], q1.at[zz * 2 + xx],
            device_id={"exp": core_peer}, device_id_type=MESH,
        )

    def r2_copy(zz):
        return pltpu.make_async_remote_copy(
            yb.at[idx(zz, 1 - x, c)], r2.at[zz], s2.at[zz], q2.at[zz],
            device_id={"exp": x_peer}, device_id_type=MESH,
        )

    def r3_dn(zz):
        return pltpu.make_async_remote_copy(
            yb.at[idx(zz, x, c)], r3.at[zz], s3.at[zz], q3u.at[zz],
            device_id={"exp": dn_peer}, device_id_type=MESH,
        )

    def r3_up(zz):
        return pltpu.make_async_remote_copy(
            yb.at[idx(zz, x, c)], r3.at[zz + 1], s3.at[zz], q3d.at[zz],
            device_id={"exp": up_peer}, device_id_type=MESH,
        )

    units = gate_up.shape[2] // 2

    def expert(zz, s):
        for xx in (0, 1):
            arrive(idx(zz, xx, 1 - c))
        rows_in = xg[pl.ds(zz * 4, 4)].reshape(4 * tokens, width)
        projected = jnp.dot(rows_in, gu[...], preferred_element_type=f32)
        gate = projected[:, :units]
        hidden = (gate / (1.0 + jnp.exp(-gate)) * projected[:, units:]).astype(bf16)
        for j in range(4):
            row = wg[zz * 4 + j, pl.ds(me, 1), :]
            column = jnp.transpose(jnp.broadcast_to(row, (8, 128)))[:tokens, :1]
            result = jnp.dot(
                hidden[j * tokens : (j + 1) * tokens], dw[...], preferred_element_type=f32
            )
            yb[zz * 4 + j] = (result.astype(bf16).astype(f32) * column).astype(bf16)
        for xx in (0, 1):
            r1_copy(zz, xx).start()

    def send_x(zz, s):
        r1_copy(zz, 1 - x).wait_recv()
        slot = idx(zz, 1 - x, c)
        yb[slot] = (yb[slot].astype(f32) + r1[zz * 2 + 1 - x].astype(f32)).astype(bf16)
        r2_copy(zz).start()

    def step(t, carry):
        both(t, own_column)

        @pl.when(t >= 1)
        def _():
            both(t - 1, other_column)

        @pl.when(t >= 2)
        def _():
            @pl.when(t == 2)
            def _():
                gu_copy.wait()
                dw_copy.wait()

            both(t - 2, expert)

        return carry

    lax.fori_loop(0, A, step, 0)
    send_x(z, 0)

    def tail(t, carry):
        @pl.when(t == A)
        def _():
            both(A - 1, other_column)

        both(t - 2, expert)
        return carry

    lax.fori_loop(A, A + 2, tail, 0)

    def scatter_x(i, carry):
        both(A - 1 - i, send_x)
        return carry

    lax.fori_loop(0, A - 1, scatter_x, 0)

    def column_sum(zz):
        r1_copy(zz, x).wait_recv()
        r2_copy(zz).wait_recv()
        return (
            yb[idx(zz, x, c)].astype(f32)
            + r1[zz * 2 + x].astype(f32)
            + r2[zz].astype(f32)
        )

    def send_z(zz, s):
        slot = idx(zz, x, c)
        base = column_sum(zz)

        def pass_on(beyond, copy, landing):
            @pl.when(beyond)
            def _():
                copy(zz).wait_recv()
                yb[slot] = (base + r3[landing].astype(f32)).astype(bf16)

            @pl.when(jnp.logical_not(beyond))
            def _():
                yb[slot] = base.astype(bf16)

            copy(zz).start()

        @pl.when(zz < z)
        def _():
            pass_on(has_up, r3_dn, zz)

        @pl.when(zz > z)
        def _():
            pass_on(has_dn, r3_up, zz + 1)

    def scatter_z(i, carry):
        both(A - 1 - i, send_z)
        return carry

    lax.fori_loop(0, A - 1, scatter_z, 0)

    mixed[...] += column_sum(z)

    @pl.when(has_up)
    def _():
        r3_dn(z).wait_recv()
        mixed[...] += r3[z].astype(f32)

    @pl.when(has_dn)
    def _():
        r3_up(z).wait_recv()
        mixed[...] += r3[z + 1].astype(f32)

    out[0] = mixed[...].astype(bf16)

    def finish(zz, carry):
        def done(copies):
            for cp in copies:
                cp.wait_send()

        @pl.when((zz <= z) & has_up)
        def _():
            done(up_copy(zz))

        @pl.when((zz >= z) & has_dn)
        def _():
            done(dn_copy(zz))

        done(x_copy(zz))
        for xx in (0, 1):
            done(core_copy(zz, xx))
            done([r1_copy(zz, xx)])
        done([r2_copy(zz)])

        @pl.when(zz < z)
        def _():
            done([r3_dn(zz)])

        @pl.when(zz > z)
        def _():
            done([r3_up(zz)])

        return carry

    lax.fori_loop(0, A, finish, 0)


def solution(mesh):
    n = mesh.shape["exp"]
    n_ctx = mesh.shape["ctx"]

    def local(
        residual, queries, key_rows, value_rows, span_order, norm_gain, gate_logits, expert_ids,
        gate_up, down_weight,
    ):
        tokens, width = residual.shape[1], residual.shape[2]
        A = n // 4
        dma = pltpu.SemaphoreType.DMA
        vmem = pl.BlockSpec(memory_space=pltpu.VMEM)
        anywhere = pl.BlockSpec(memory_space=pl.ANY)
        block = lambda count: pltpu.VMEM((count, tokens, width), bf16)
        return pl.pallas_call(
            functools.partial(kernel, n, n_ctx),
            out_shape=jax.ShapeDtypeStruct(residual.shape, bf16),
            in_specs=[vmem] * 4
            + [pl.BlockSpec(memory_space=pltpu.SMEM)]
            + [vmem] * 3
            + [anywhere] * 2,
            out_specs=vmem,
            scratch_shapes=[
                pltpu.VMEM((n_ctx,) + key_rows.shape[1:], bf16),
                pltpu.VMEM((n_ctx,) + value_rows.shape[1:], bf16),
                pltpu.VMEM((tokens, width), f32),
                block(n),
                pltpu.VMEM((n, n, 128), f32),
                block(n),
                block(2 * A),
                block(A),
                block(A + 1),
                pltpu.VMEM(gate_up.shape[1:], bf16),
                pltpu.VMEM(down_weight.shape[1:], bf16),
                dma((2,)),
                dma((2, n_ctx)),
                dma((2, n_ctx)),
                dma((5 * A,)),
                dma((n,)),
                dma((5 * A,)),
                dma((n,)),
                dma((2 * A,)),
                dma((2 * A,)),
                dma((A,)),
                dma((A,)),
                dma((A,)),
                dma((A,)),
                dma((A,)),
            ],
            compiler_params=pltpu.CompilerParams(
                collective_id=0, has_side_effects=True, vmem_limit_bytes=67043328
            ),
        )(
            residual, queries, key_rows, value_rows, span_order, norm_gain[None], gate_logits,
            expert_ids, gate_up, down_weight,
        )

    return jax.shard_map(
        local,
        mesh=mesh,
        in_specs=(
            P("exp", "ctx", None),
            P("exp", "ctx", None),
            P("exp", "ctx", None),
            P("exp", "ctx", None),
            P(),
            P(),
            P("exp", "ctx", None),
            P("exp", "ctx", None),
            P("exp", None, None),
            P("exp", None, None),
        ),
        out_specs=P("exp", "ctx", None),
        check_vma=False,
    )
```

time: 145 us -> 79.1 us (0.55)
  the two profiles are of different devices: /device:TPU:11 before, /device:TPU:0 now
where the time goes in v1:
time: 79.1 us; the launch traced here: 78.9 us
  Pallas kernels  74.5 us (94%)
  local copies, waits for them, and re-layouts  4.42 us (6%)
    pallas_call x1, Pallas kernels, local(): pl.pallas_call(functools.partial(kernel, n, n_ctx), out_shape=jax.ShapeDt...  74.5 us
    unnamed x3, local copies, waits for them, and re-layouts  4.42 us

profile of v1, /device:TPU:0, one launch (start us, length us, event | category | flops | bytes accessed | tf_op | source)
XLA Modules:
  0.0 78.9 jit_solution(16050090438463525850)
XLA Ops:
  0.0 1.4 %copy.11.gate_logits = f32[1,64,8]{2,1,0:T(8,128)} copy(f32[1,64,8]{1,2,0:T(8,128)} %param.16) | data formatting | bytes 4096 | tf_op args[6]
  1.4 1.4 %copy.12.expert_ids = s32[1,64,8]{2,1,0:T(8,128)} copy(s32[1,64,8]{1,2,0:T(8,128)} %param.17) | data formatting | bytes 4096 | tf_op args[7]
  2.8 74.5 %shard_map.100 = bf16[1,64,2048]{2,1,0:T(8,128)(2,1)} custom-call(bf16[1,64,2048]{2,1,0:T(8,128)(2,1)} %residual.1, bf16[1,64,2048]{2,1,0:T(8,128)(2,1)} %queries.1, bf16[1,64,256]{2,1,0:T(8,128)(2,1)} %key_rows.1, bf16[1,64,256]{2,1,0:T(8,128)(2,1)} %value_rows.1, s32[4]{0:T(128)} %span_order.1, f32[1,2048]{1,0:T(1,128)} %bitcast.1, ...), custom_call_target="tpu_custom_call" | custom-call | tf_op jit(solution)/shard_map/pallas_call | solution.py:385
  77.3 1.7 %copy.14 = bf16[1,64,2048]{2,1,0:T(8,128)(2,1)} copy(bf16[1,64,2048]{2,1,0:T(8,128)(2,1)} %shard_map.100) | data formatting | bytes 524288

commit v2 on v1

v2 whole, which is shorter than its diff:
```python
import functools
import math

import jax
import jax.numpy as jnp
from jax import lax
from jax.experimental import pallas as pl
from jax.experimental.pallas import tpu as pltpu
from jax.sharding import PartitionSpec as P

MESH = pl.DeviceIdType.MESH
HD = 128
big_negative = -1e30
norm_eps = 1e-06
f32 = jnp.float32
bf16 = jnp.bfloat16


def block_positions(span_ref, row_index, rows_per_span):
    which = row_index // rows_per_span
    start = jnp.zeros_like(row_index)
    for b in range(span_ref.shape[0]):
        start = jnp.where(which == b, span_ref[b], start)
    return start * rows_per_span + row_index % rows_per_span


def kernel(
    n, n_ctx,
    residual, queries, key_rows, value_rows, span_order, norm_gain, gate_logits, expert_ids,
    gate_up, down_weight,
    out,
    keys, values, mixed, xg, wg, yb, r1, r2, r3, extra, acc, gu, dw,
    wsem, kv_send, kv_recv, gs, gr, ws, wr, s1, q1, s2, q2, s3, q3u, q3d, se, qe,
):
    A = n // 4
    tokens = residual.shape[1]
    width = residual.shape[2]
    kvh = key_rows.shape[2] // HD
    group = width // HD // kvh
    me = lax.axis_index("exp")
    ctx = lax.axis_index("ctx")
    c = me % 2
    x = (me // 2) % 2
    z = me // 4

    def idx(zz, xx, cc):
        return (zz * 2 + xx) * 2 + cc

    core_peer = idx(z, x, 1 - c)
    x_peer = idx(z, 1 - x, c)
    up_peer = jnp.minimum(z + 1, A - 1) * 4 + x * 2 + c
    dn_peer = jnp.maximum(z - 1, 0) * 4 + x * 2 + c
    half = tokens // 2
    pair = z + 1 - 2 * (z % 2)
    pair_peer = idx(pair, x, c)
    detour = (A - 1) * (1 - z % 2)
    pair_detour = (A - 1) * (z % 2)
    has_up = z < A - 1
    has_dn = z > 0

    gu_copy = pltpu.make_async_copy(gate_up.at[0], gu, wsem.at[0])
    dw_copy = pltpu.make_async_copy(down_weight.at[0], dw, wsem.at[1])
    gu_copy.start()
    dw_copy.start()

    barrier = pltpu.get_barrier_semaphore()
    for k in range(1, n_ctx):
        pl.semaphore_signal(
            barrier, inc=1, device_id={"ctx": (ctx + k) % n_ctx}, device_id_type=MESH
        )
    for peer in (core_peer, x_peer):
        pl.semaphore_signal(barrier, inc=1, device_id={"exp": peer}, device_id_type=MESH)

    @pl.when(has_up)
    def _():
        pl.semaphore_signal(barrier, inc=1, device_id={"exp": up_peer}, device_id_type=MESH)

    @pl.when(has_dn)
    def _():
        pl.semaphore_signal(barrier, inc=1, device_id={"exp": dn_peer}, device_id_type=MESH)

    pl.semaphore_wait(barrier, n_ctx + 1 + jnp.where(has_up, 1, 0) + jnp.where(has_dn, 1, 0))

    def kv_copies(k):
        target = {"ctx": (ctx + k) % n_ctx}
        return [
            pltpu.make_async_remote_copy(
                src.at[0], dst.at[ctx], kv_send.at[i, k], kv_recv.at[i, k],
                device_id=target, device_id_type=MESH,
            )
            for i, (src, dst) in enumerate(((key_rows, keys), (value_rows, values)))
        ]

    for k in range(1, n_ctx):
        for cp in kv_copies(k):
            cp.start()
    keys[ctx] = key_rows[0]
    values[ctx] = value_rows[0]

    raised = jnp.exp(gate_logits[0])
    routing = raised / jnp.sum(raised, axis=0, keepdims=True)
    experts = lax.broadcasted_iota(jnp.int32, (n, tokens), 0)
    dense = jnp.zeros((n, tokens), f32)
    for j in range(routing.shape[0]):
        dense = jnp.where(expert_ids[0][j : j + 1] == experts, routing[j : j + 1], dense)
    wg[me] = jnp.zeros((n, 128), f32)
    wg[me, :, :tokens] = dense

    total_keys = n_ctx * tokens
    rows_per_span = total_keys // span_order.shape[0]
    query_pos = block_positions(
        span_order, ctx * tokens + lax.broadcasted_iota(jnp.int32, (tokens, 1), 0), rows_per_span
    )
    key_pos = block_positions(
        span_order, lax.broadcasted_iota(jnp.int32, (1, total_keys), 1), rows_per_span
    )
    visible = jnp.where(key_pos <= query_pos, 1, 0)
    visible = jnp.concatenate([visible] * group, axis=0) > 0

    for k in range(1, n_ctx):
        for cp in kv_copies(k):
            cp.wait()

    for g in range(kvh):
        heads = [g * group + i for i in range(group)]
        q = jnp.concatenate([queries[0, :, h * HD : (h + 1) * HD] for h in heads], axis=0)
        kk = keys[:, :, g * HD : (g + 1) * HD].reshape(total_keys, HD)
        vv = values[:, :, g * HD : (g + 1) * HD].reshape(total_keys, HD)
        scores = lax.dot_general(
            q, kk, (((1,), (1,)), ((), ())), preferred_element_type=f32
        ) * (1.0 / math.sqrt(HD))
        scores = jnp.where(visible, scores, big_negative)
        weights = jnp.where(
            visible, jnp.exp(scores - jnp.max(scores, axis=1, keepdims=True)), 0.0
        )
        total = jnp.sum(weights, axis=1, keepdims=True)
        summed = jnp.dot(weights.astype(bf16), vv, preferred_element_type=f32) / total
        summed = summed.astype(bf16).astype(f32)
        for i, h in enumerate(heads):
            cols = slice(h * HD, (h + 1) * HD)
            mixed[:, cols] = (
                residual[0, :, cols].astype(f32) + summed[i * tokens : (i + 1) * tokens]
            )

    rows = mixed[...]
    scale = lax.rsqrt(jnp.mean(rows * rows, axis=1, keepdims=True) + norm_eps)
    normed = (rows * scale * norm_gain[...]).astype(bf16)
    for h in (0, 1):
        xg[me * 2 + h] = normed[h * half : (h + 1) * half]

    def unit(slot, h, target, k):
        return pltpu.make_async_remote_copy(
            xg.at[slot * 2 + h], xg.at[slot * 2 + h], gs.at[k * 2 + h], gr.at[slot * 2 + h],
            device_id={"exp": target}, device_id_type=MESH,
        )

    def routes(slot, target, k):
        return pltpu.make_async_remote_copy(
            wg.at[slot], wg.at[slot], ws.at[k], wr.at[slot],
            device_id={"exp": target}, device_id_type=MESH,
        )

    def relay(slot, h, target, k):
        unit(slot, h, target, k).start()

        @pl.when(h == 0)
        def _():
            routes(slot, target, k).start()

    def arrive(slot, h):
        unit(slot, h, core_peer, 0).wait_recv()

        @pl.when(h == 0)
        def _():
            routes(slot, core_peer, 0).wait_recv()

    def both(t, body):
        def one(s, carry):
            zz = z + t * (1 - 2 * s)
            ok = (zz >= 0) & (zz < A) & ((t > 0) | (s == 0))

            @pl.when(ok)
            def _():
                body(zz)

            return carry

        lax.fori_loop(0, 2, one, 0)

    def own_column(zz, h):
        slot = idx(zz, x, c)

        @pl.when(zz != z)
        def _():
            arrive(slot, h)

        @pl.when((zz <= z) & has_up)
        def _():
            relay(slot, h, up_peer, zz)

        @pl.when((zz >= z) & has_dn)
        def _():
            relay(slot, h, dn_peer, A + zz)

        @pl.when((zz != detour) | (h == 1))
        def _():
            unit(slot, h, x_peer, 2 * A + zz).start()

        @pl.when(h == 0)
        def _():
            routes(slot, x_peer, 2 * A + zz).start()

        relay(slot, h, core_peer, 3 * A + zz * 2 + x)

    def detour_copy():
        slot = idx(pair_detour, 1 - x, c)
        return pltpu.make_async_remote_copy(
            xg.at[slot * 2], xg.at[slot * 2], se.at[0], gr.at[slot * 2],
            device_id={"exp": pair_peer}, device_id_type=MESH,
        )

    def other_column(zz, h):
        slot = idx(zz, 1 - x, c)
        arrive(slot, h)

        @pl.when((zz == pair_detour) & (h == 0))
        def _():
            detour_copy().start()

        relay(slot, h, core_peer, 3 * A + zz * 2 + 1 - x)

    def r1_copy(zz, xx):
        return pltpu.make_async_remote_copy(
            yb.at[pl.ds(idx(zz, xx, 1 - c) * 2, 2)], r1.at[pl.ds((zz * 2 + xx) * 2, 2)],
            s1.at[zz * 2 + xx], q1.at[zz * 2 + xx],
            device_id={"exp": core_peer}, device_id_type=MESH,
        )

    def r2_copy(zz, h):
        k = zz * 2 + h
        return pltpu.make_async_remote_copy(
            yb.at[idx(zz, 1 - x, c) * 2 + h], r2.at[k], s2.at[k], q2.at[k],
            device_id={"exp": x_peer}, device_id_type=MESH,
        )

    def extra_copy():
        return pltpu.make_async_remote_copy(
            yb.at[idx(detour, 1 - x, c) * 2], extra, se.at[1], qe.at[0],
            device_id={"exp": pair_peer}, device_id_type=MESH,
        )

    def r3_dn(zz, h):
        k = zz * 2 + h
        return pltpu.make_async_remote_copy(
            yb.at[idx(zz, x, c) * 2 + h], r3.at[k], s3.at[k], q3u.at[k],
            device_id={"exp": dn_peer}, device_id_type=MESH,
        )

    def r3_up(zz, h):
        k = zz * 2 + h
        return pltpu.make_async_remote_copy(
            yb.at[idx(zz, x, c) * 2 + h], r3.at[k + 2], s3.at[k], q3d.at[k],
            device_id={"exp": up_peer}, device_id_type=MESH,
        )

    units = gate_up.shape[2] // 2

    def expert(zz, xx):
        for h in (0, 1):
            unit(idx(zz, xx, 1 - c), h, core_peer, 0).wait_recv()
        routes(idx(zz, xx, 1 - c), core_peer, 0).wait_recv()
        first = zz * 4 + xx * 2
        rows_in = xg[pl.ds(first * 2, 4)].reshape(2 * tokens, width)
        projected = jnp.dot(rows_in, gu[...], preferred_element_type=f32)
        gate = projected[:, :units]
        hidden = (gate / (1.0 + jnp.exp(-gate)) * projected[:, units:]).astype(bf16)
        result = jnp.dot(hidden, dw[...], preferred_element_type=f32)
        for j in (0, 1):
            row = wg[first + j, pl.ds(me, 1), :]
            column = jnp.transpose(jnp.broadcast_to(row, (8, 128)))[:tokens, :1]
            scaled = (
                result[j * tokens : (j + 1) * tokens].astype(bf16).astype(f32) * column
            ).astype(bf16)
            for h in (0, 1):
                yb[(first + j) * 2 + h] = scaled[h * half : (h + 1) * half]
        r1_copy(zz, xx).start()

    def send_x(zz, h):
        @pl.when(h == 1)
        def _():
            r1_copy(zz, 1 - x).wait_recv()

        k = idx(zz, 1 - x, c) * 2 + h
        acc[...] = yb[k].astype(f32) + r1[(zz * 2 + 1 - x) * 2 + h].astype(f32)

        @pl.when((zz == pair_detour) & (h == 0))
        def _():
            extra_copy().wait_recv()
            acc[...] += extra[...].astype(f32)

        yb[k] = acc[...].astype(bf16)
        around = (zz == detour) & (h == 0)

        @pl.when(around)
        def _():
            extra_copy().start()

        @pl.when(jnp.logical_not(around))
        def _():
            r2_copy(zz, h).start()

    def step(u, carry):
        t, h = u // 2, u % 2
        both(t, lambda zz: own_column(zz, h))

        @pl.when(u >= 1)
        def _():
            both((u - 1) // 2, lambda zz: other_column(zz, (u - 1) % 2))

        @pl.when(u >= 2)
        def _():
            @pl.when(u == 2)
            def _():
                gu_copy.wait()
                dw_copy.wait()

            both(t - 1, lambda zz: expert(zz, jnp.where(h == 0, x, 1 - x)))

        return carry

    lax.fori_loop(0, 2 * A, step, 0)
    send_x(z, 1)

    def tail(i, carry):
        @pl.when(i == 1)
        def _():
            both(A - 1, lambda zz: other_column(zz, 1))

        both(A - 1, lambda zz: expert(zz, jnp.where(i == 0, x, 1 - x)))
        return carry

    lax.fori_loop(0, 2, tail, 0)

    def scatter_x(i, carry):
        both(A - 1 - i // 2, lambda zz: send_x(zz, 1 - i % 2))
        return carry

    lax.fori_loop(0, 2 * (A - 1), scatter_x, 0)
    send_x(z, 0)

    def column_sum(zz, h):
        @pl.when(h == 1)
        def _():
            r1_copy(zz, x).wait_recv()

        acc[...] = yb[idx(zz, x, c) * 2 + h].astype(f32) + r1[(zz * 2 + x) * 2 + h].astype(f32)

        @pl.when((zz != detour) | (h == 1))
        def _():
            r2_copy(zz, h).wait_recv()
            acc[...] += r2[zz * 2 + h].astype(f32)

        @pl.when((zz <= z) & has_up)
        def _():
            r3_dn(zz, h).wait_recv()
            acc[...] += r3[zz * 2 + h].astype(f32)

        @pl.when((zz >= z) & has_dn)
        def _():
            r3_up(zz, h).wait_recv()
            acc[...] += r3[zz * 2 + 2 + h].astype(f32)

    def send_z(zz, h):
        column_sum(zz, h)
        yb[idx(zz, x, c) * 2 + h] = acc[...].astype(bf16)

        @pl.when(zz < z)
        def _():
            r3_dn(zz, h).start()

        @pl.when(zz > z)
        def _():
            r3_up(zz, h).start()

    def scatter_z(i, carry):
        both(A - 1 - i // 2, lambda zz: send_z(zz, 1 - i % 2))
        return carry

    lax.fori_loop(0, 2 * (A - 1), scatter_z, 0)

    for h in (1, 0):
        column_sum(z, h)
        part = slice(h * half, (h + 1) * half)
        out[0, part] = (mixed[part] + acc[...]).astype(bf16)

    def finish(zz, carry):
        slot = idx(zz, x, c)

        def done(slot, target, k):
            for h in (0, 1):
                unit(slot, h, target, k).wait_send()
            routes(slot, target, k).wait_send()

        @pl.when((zz <= z) & has_up)
        def _():
            done(slot, up_peer, zz)

        @pl.when((zz >= z) & has_dn)
        def _():
            done(slot, dn_peer, A + zz)

        @pl.when(zz != detour)
        def _():
            unit(slot, 0, x_peer, 2 * A + zz).wait_send()
            r2_copy(zz, 0).wait_send()

        unit(slot, 1, x_peer, 2 * A + zz).wait_send()
        r2_copy(zz, 1).wait_send()
        routes(slot, x_peer, 2 * A + zz).wait_send()
        for xx in (0, 1):
            done(idx(zz, xx, c), core_peer, 3 * A + zz * 2 + xx)
            r1_copy(zz, xx).wait_send()

        @pl.when(zz < z)
        def _():
            for h in (0, 1):
                r3_dn(zz, h).wait_send()

        @pl.when(zz > z)
        def _():
            for h in (0, 1):
                r3_up(zz, h).wait_send()

        return carry

    lax.fori_loop(0, A, finish, 0)
    detour_copy().wait_send()
    extra_copy().wait_send()


def solution(mesh):
    n = mesh.shape["exp"]
    n_ctx = mesh.shape["ctx"]

    def local(
        residual, queries, key_rows, value_rows, span_order, norm_gain, gate_logits, expert_ids,
        gate_up, down_weight,
    ):
        tokens, width = residual.shape[1], residual.shape[2]
        A = n // 4
        dma = pltpu.SemaphoreType.DMA
        vmem = pl.BlockSpec(memory_space=pltpu.VMEM)
        anywhere = pl.BlockSpec(memory_space=pl.ANY)
        block = lambda count: pltpu.VMEM((count * 2, tokens // 2, width), bf16)
        return pl.pallas_call(
            functools.partial(kernel, n, n_ctx),
            out_shape=jax.ShapeDtypeStruct(residual.shape, bf16),
            in_specs=[vmem] * 4
            + [pl.BlockSpec(memory_space=pltpu.SMEM)]
            + [vmem] * 3
            + [anywhere] * 2,
            out_specs=vmem,
            scratch_shapes=[
                pltpu.VMEM((n_ctx,) + key_rows.shape[1:], bf16),
                pltpu.VMEM((n_ctx,) + value_rows.shape[1:], bf16),
                pltpu.VMEM((tokens, width), f32),
                block(n),
                pltpu.VMEM((n, n, 128), f32),
                block(n),
                block(2 * A),
                block(A),
                block(A + 1),
                pltpu.VMEM((tokens // 2, width), bf16),
                pltpu.VMEM((tokens // 2, width), f32),
                pltpu.VMEM(gate_up.shape[1:], bf16),
                pltpu.VMEM(down_weight.shape[1:], bf16),
                dma((2,)),
                dma((2, n_ctx)),
                dma((2, n_ctx)),
                dma((10 * A,)),
                dma((2 * n,)),
                dma((5 * A,)),
                dma((n,)),
                dma((2 * A,)),
                dma((2 * A,)),
                dma((2 * A,)),
                dma((2 * A,)),
                dma((2 * A,)),
                dma((2 * A,)),
                dma((2 * A,)),
                dma((2,)),
                dma((1,)),
            ],
            compiler_params=pltpu.CompilerParams(
                collective_id=0, has_side_effects=True, vmem_limit_bytes=67043328
            ),
        )(
            residual, queries, key_rows, value_rows, span_order, norm_gain[None],
            jnp.swapaxes(gate_logits, 1, 2), jnp.swapaxes(expert_ids, 1, 2), gate_up, down_weight,
        )

    return jax.shard_map(
        local,
        mesh=mesh,
        in_specs=(
            P("exp", "ctx", None),
            P("exp", "ctx", None),
            P("exp", "ctx", None),
            P("exp", "ctx", None),
            P(),
            P(),
            P("exp", "ctx", None),
            P("exp", "ctx", None),
            P("exp", None, None),
            P("exp", None, None),
        ),
        out_specs=P("exp", "ctx", None),
        check_vma=False,
    )
```

time: 79.1 us -> 71.5 us (0.904)
  Pallas kernels: 74.5 us -> 69.7 us
  local copies, waits for them, and re-layouts: 4.42 us -> 1.67 us
    pallas_call x1, Pallas kernels: 74.5 us -> 69.7 us  [local(): pl.pallas_call(functools.partial(kernel, n, n_ctx), out_shape=jax.ShapeDt...]
    unnamed x3 -> x1, local copies, waits for them, and re-layouts: 4.42 us -> 1.67 us
where the time goes in v2:
time: 71.5 us; the launch traced here: 71.4 us
  Pallas kernels  69.7 us (97%)
  local copies, waits for them, and re-layouts  1.67 us (2%)
    pallas_call x1, Pallas kernels, local(): pl.pallas_call(functools.partial(kernel, n, n_ctx), out_shape=jax.ShapeDt...  69.7 us
    unnamed x1, local copies, waits for them, and re-layouts  1.67 us

profile of v2, /device:TPU:0, one launch (start us, length us, event | category | flops | bytes accessed | tf_op | source)
XLA Modules:
  0.0 71.4 jit_solution(2066387595208058216)
XLA Ops:
  0.0 69.7 %shard_map.100 = bf16[1,64,2048]{2,1,0:T(8,128)(2,1)} custom-call(bf16[1,64,2048]{2,1,0:T(8,128)(2,1)} %residual.1, bf16[1,64,2048]{2,1,0:T(8,128)(2,1)} %queries.1, bf16[1,64,256]{2,1,0:T(8,128)(2,1)} %key_rows.1, bf16[1,64,256]{2,1,0:T(8,128)(2,1)} %value_rows.1, s32[4]{0:T(128)} %span_order.1, f32[1,2048]{1,0:T(1,128)} %bitcast.3, f32[1,8,64]{2,1,0:T(8,128)} %bitcast.4, ...), custom_call_target="tpu_custom_call" | custom-call | tf_op jit(solution)/shard_map/pallas_call | solution.py:455
  69.7 1.7 %copy.12 = bf16[1,64,2048]{2,1,0:T(8,128)(2,1)} copy(bf16[1,64,2048]{2,1,0:T(8,128)(2,1)} %shard_map.100) | data formatting | bytes 524288

commit v3 on v2

--- a/solution.py
+++ b/solution.py
@@ -26,9 +26,10 @@
 
 def kernel(
     n, n_ctx,
-    residual, queries, key_rows, value_rows, span_order, norm_gain, gate_logits, expert_ids,
+    residual_in, queries_in, key_rows, value_rows, span_order, norm_gain, gate_logits, expert_ids,
     gate_up, down_weight,
     out,
+    residual, queries,
     keys, values, mixed, xg, wg, yb, r1, r2, r3, extra, acc, gu, dw,
     wsem, kv_send, kv_recv, gs, gr, ws, wr, s1, q1, s2, q2, s3, q3u, q3d, se, qe,
 ):
@@ -58,11 +59,6 @@
     has_up = z < A - 1
     has_dn = z > 0
 
-    gu_copy = pltpu.make_async_copy(gate_up.at[0], gu, wsem.at[0])
-    dw_copy = pltpu.make_async_copy(down_weight.at[0], dw, wsem.at[1])
-    gu_copy.start()
-    dw_copy.start()
-
     barrier = pltpu.get_barrier_semaphore()
     for k in range(1, n_ctx):
         pl.semaphore_signal(
@@ -79,6 +75,16 @@
     def _():
         pl.semaphore_signal(barrier, inc=1, device_id={"exp": dn_peer}, device_id_type=MESH)
 
+    loads = [
+        pltpu.make_async_copy(queries_in, queries, wsem.at[0]),
+        pltpu.make_async_copy(residual_in, residual, wsem.at[1]),
+    ]
+    gu_copy = pltpu.make_async_copy(gate_up.at[0], gu, wsem.at[2])
+    dw_copy = pltpu.make_async_copy(down_weight.at[0], dw, wsem.at[3])
+    for cp in loads:
+        cp.start()
+    gu_copy.start()
+    dw_copy.start()
     pl.semaphore_wait(barrier, n_ctx + 1 + jnp.where(has_up, 1, 0) + jnp.where(has_dn, 1, 0))
 
     def kv_copies(k):
@@ -117,6 +123,8 @@
     visible = jnp.where(key_pos <= query_pos, 1, 0)
     visible = jnp.concatenate([visible] * group, axis=0) > 0
 
+    for cp in loads:
+        cp.wait()
     for k in range(1, n_ctx):
         for cp in kv_copies(k):
             cp.wait()
@@ -346,7 +354,6 @@
         return carry
 
     lax.fori_loop(0, 2 * (A - 1), scatter_x, 0)
-    send_x(z, 0)
 
     def column_sum(zz, h):
         @pl.when(h == 1)
@@ -386,7 +393,9 @@
         both(A - 1 - i // 2, lambda zz: send_z(zz, 1 - i % 2))
         return carry
 
-    lax.fori_loop(0, 2 * (A - 1), scatter_z, 0)
+    lax.fori_loop(0, A - 1, scatter_z, 0)
+    send_x(z, 0)
+    lax.fori_loop(A - 1, 2 * (A - 1), scatter_z, 0)
 
     for h in (1, 0):
         column_sum(z, h)
@@ -455,12 +464,15 @@
         return pl.pallas_call(
             functools.partial(kernel, n, n_ctx),
             out_shape=jax.ShapeDtypeStruct(residual.shape, bf16),
-            in_specs=[vmem] * 4
+            in_specs=[anywhere] * 2
+            + [vmem] * 2
             + [pl.BlockSpec(memory_space=pltpu.SMEM)]
             + [vmem] * 3
             + [anywhere] * 2,
             out_specs=vmem,
             scratch_shapes=[
+                pltpu.VMEM(residual.shape, bf16),
+                pltpu.VMEM(queries.shape, bf16),
                 pltpu.VMEM((n_ctx,) + key_rows.shape[1:], bf16),
                 pltpu.VMEM((n_ctx,) + value_rows.shape[1:], bf16),
                 pltpu.VMEM((tokens, width), f32),
@@ -474,7 +486,7 @@
                 pltpu.VMEM((tokens // 2, width), f32),
                 pltpu.VMEM(gate_up.shape[1:], bf16),
                 pltpu.VMEM(down_weight.shape[1:], bf16),
-                dma((2,)),
+                dma((4,)),
                 dma((2, n_ctx)),
                 dma((2, n_ctx)),
                 dma((10 * A,)),

time: 71.5 us -> 67.4 us (0.943)
  Pallas kernels: 69.7 us -> 65.5 us
    pallas_call x1, Pallas kernels: 69.7 us -> 65.5 us  [local(): pl.pallas_call(functools.partial(kernel, n, n_ctx), out_shape=jax.ShapeDt...]
where the time goes in v3:
time: 67.4 us; the launch traced here: 67.1 us
  Pallas kernels  65.5 us (97%)
  local copies, waits for them, and re-layouts  1.67 us (2%)
    pallas_call x1, Pallas kernels, local(): pl.pallas_call(functools.partial(kernel, n, n_ctx), out_shape=jax.ShapeDt...  65.5 us
    unnamed x1, local copies, waits for them, and re-layouts  1.67 us

profile of v3, /device:TPU:0, one launch (start us, length us, event | category | flops | bytes accessed | tf_op | source)
XLA Modules:
  0.0 67.1 jit_solution(10577034717329735747)
XLA Ops:
  0.0 65.5 %shard_map.100 = bf16[1,64,2048]{2,1,0:T(8,128)(2,1)} custom-call(bf16[1,64,2048]{2,1,0:T(8,128)(2,1)} %residual_in.1, bf16[1,64,2048]{2,1,0:T(8,128)(2,1)} %queries_in.1, bf16[1,64,256]{2,1,0:T(8,128)(2,1)} %key_rows.1, bf16[1,64,256]{2,1,0:T(8,128)(2,1)} %value_rows.1, s32[4]{0:T(128)} %span_order.1, f32[1,2048]{1,0:T(1,128)} %bitcast.3, ...), custom_call_target="tpu_custom_call" | custom-call | tf_op jit(solution)/shard_map/pallas_call | solution.py:464
  65.5 1.7 %copy.12 = bf16[1,64,2048]{2,1,0:T(8,128)(2,1)} copy(bf16[1,64,2048]{2,1,0:T(8,128)(2,1)} %shard_map.100) | data formatting | bytes 524288
